TPU v7x, 32 devices: a whole 2x2x4 slice. The times are simulated.
32 devices in a mesh: fsdp: 8 (over z, y), seq: 4 (over x, core).
Axes of the slice: x: 2, y: 2, z: 4, core: 2. Of those that a mesh axis runs over, the one named last changes fastest.
Arguments:
- layer_input: bfloat16 [4096, 2048], P(('fsdp', 'seq')), may hold values from -6 to 6
- segment_ids: int32 [8, 512], P('fsdp'), may hold values from 0 to 7, as said below
- positions: int32 [4096], P('fsdp'), may hold values from 0 to 766, as said below
- ln1_gain: bfloat16 [2048], P(('fsdp', 'seq')), may hold values from 0.5 to 1.5
- ln1_bias: bfloat16 [2048], P(('fsdp', 'seq')), may hold values from -4 to 4
- qkv_weight: bfloat16 [2048, 6144], P(('fsdp', 'seq')), may hold values from -0.125 to 0.125
- qkv_bias: bfloat16 [6144], P(('fsdp', 'seq')), may hold values from -6 to 6
- out_weight: bfloat16 [2048, 2048], P(('fsdp', 'seq')), may hold values from -0.75 to 0.75
- ln2_gain: bfloat16 [2048], P(('fsdp', 'seq')), may hold values from 0.5 to 1.5
- ln2_bias: bfloat16 [2048], P(('fsdp', 'seq')), may hold values from -4 to 4
- gate_weight: bfloat16 [2048, 5632], P(('fsdp', 'seq')), may hold values from -0.125 to 0.125
- up_weight: bfloat16 [2048, 5632], P(('fsdp', 'seq')), may hold values from -0.125 to 0.125
- down_weight: bfloat16 [2048, 5632], P(('fsdp', 'seq')), may hold values from -0.078125 to 0.078125
- cotangent: bfloat16 [4096, 2048], P(('fsdp', 'seq')), may hold values from -6 to 6
Outputs:
- layer_output: bfloat16 [4096, 2048], P(('fsdp', 'seq'))
- input_grad: float32 [4096, 2048], P(('fsdp', 'seq'))
- ln1_gain_grad: float32 [2048], P(('fsdp', 'seq'))
- ln1_bias_grad: float32 [2048], P(('fsdp', 'seq'))
- qkv_weight_grad: float32 [2048, 6144], P(('fsdp', 'seq'))
- qkv_bias_grad: float32 [6144], P(('fsdp', 'seq'))
- out_weight_grad: float32 [2048, 2048], P(('fsdp', 'seq'))
- ln2_gain_grad: float32 [2048], P(('fsdp', 'seq'))
- ln2_bias_grad: float32 [2048], P(('fsdp', 'seq'))
- gate_weight_grad: float32 [2048, 5632], P(('fsdp', 'seq'))
- up_weight_grad: float32 [2048, 5632], P(('fsdp', 'seq'))
- down_weight_grad: float32 [2048, 5632], P(('fsdp', 'seq'))
Inputs may be any that keep to these rules, and one draw needn't show every extreme that they name: `segment_ids`: segment ids never fall along a sequence; each document holds 64 to 256 tokens, the first and last of a sequence may be cut. `positions`: A token's position counts from its document's first token, which for a sequence's first document may lie up to 511 tokens before the sequence.
All inputs are finite; a program needn't handle non-finite values.
Results may differ from a plain program's by a relative error of at most 0.012.
Values may be sent and summed in bfloat16 or wider, within the bound.
No kernel may reach another device: no remote copies, remote signals or barrier semaphores. Data moves between devices by JAX's collectives and lax.ppermute only.
A program may use at most 256 MiB of HBM per device.

v0:
```python
import jax
import jax.numpy as jnp
from jax import lax
from jax.sharding import PartitionSpec as P

HEADS = 32
HEAD_DIM = 64


def layer_norm(values, gain, shift):
    center = jnp.mean(values, axis=-1, keepdims=True)
    centered = values - center
    spread = jnp.mean(centered * centered, axis=-1, keepdims=True)
    return centered * lax.rsqrt(spread + 1e-05) * gain + shift


def rotary_tables(spots):
    inverse = 10000.0 ** (-jnp.arange(8).astype(jnp.float32) / 8.0)
    angle = spots.astype(jnp.float32)[:, None] * inverse[None, :]
    return (jnp.cos(angle), jnp.sin(angle))


def rotate(heads_view, cosine, sine):
    first = heads_view[..., :8]
    second = heads_view[..., 8:16]
    rest = heads_view[..., 16:]
    cos_part = cosine[:, None, :]
    sin_part = sine[:, None, :]
    return jnp.concatenate(
        [first * cos_part - second * sin_part, second * cos_part + first * sin_part, rest], axis=-1
    )


def contract_rows(left, right):
    return lax.dot_general(
        left, right, (((0,), (0,)), ((), ())), preferred_element_type=jnp.float32
    )


def contract_cols(left, right):
    return lax.dot_general(
        left, right, (((1,), (1,)), ((), ())), preferred_element_type=jnp.float32
    )


def swiglu(gate, up):
    return jax.nn.silu(gate) * up


def fetch_all(first, second, third, fourth, fifth):
    return (
        lax.all_gather(first, ("fsdp", "seq"), axis=0, tiled=True),
        lax.all_gather(second, ("fsdp", "seq"), axis=0, tiled=True),
        lax.all_gather(third, ("fsdp", "seq"), axis=0, tiled=True),
        lax.all_gather(fourth, ("fsdp", "seq"), axis=0, tiled=True),
        lax.all_gather(fifth, ("fsdp", "seq"), axis=0, tiled=True),
    )


def sum_all(first, second, third, fourth, fifth):
    return (
        lax.psum_scatter(first, ("fsdp", "seq"), scatter_dimension=0, tiled=True),
        lax.psum_scatter(second, ("fsdp", "seq"), scatter_dimension=0, tiled=True),
        lax.psum_scatter(third, ("fsdp", "seq"), scatter_dimension=0, tiled=True),
        lax.psum_scatter(fourth, ("fsdp", "seq"), scatter_dimension=0, tiled=True),
        lax.psum_scatter(fifth, ("fsdp", "seq"), scatter_dimension=0, tiled=True),
    )


def fetch_block(first, second):
    columns = (
        lax.all_to_all(first, "seq", split_axis=2, concat_axis=0, tiled=True),
        lax.all_to_all(second, "seq", split_axis=2, concat_axis=0, tiled=True),
    )
    return (
        lax.all_gather(columns[0], "fsdp", axis=0, tiled=True),
        lax.all_gather(columns[1], "fsdp", axis=0, tiled=True),
    )


def return_block(first, second):
    summed = (
        lax.psum_scatter(first, "fsdp", scatter_dimension=0, tiled=True),
        lax.psum_scatter(second, "fsdp", scatter_dimension=0, tiled=True),
    )
    return (
        lax.all_to_all(summed[0], "seq", split_axis=0, concat_axis=2, tiled=True),
        lax.all_to_all(summed[1], "seq", split_axis=0, concat_axis=2, tiled=True),
    )


def seq_rows(values):
    return lax.all_gather(values, "seq", axis=0, tiled=True)


def seq_sums(values):
    return lax.psum_scatter(values, "seq", scatter_dimension=0, tiled=True)


def split_heads(
    layer_input,
    segment_ids,
    positions,
    ln1_gain,
    ln1_bias,
    qkv_weight,
    qkv_bias,
    out_weight,
    ln2_gain,
    ln2_bias,
    gate_weight,
    up_weight,
    down_weight,
    cotangent,
):
    width = layer_input.shape[1]
    own_rows = qkv_weight.shape[0]
    hidden_units = gate_weight.shape[1]
    quarter = lax.axis_size("seq")
    seq_spot = lax.axis_index("seq")
    width_part = width // quarter
    units_part = hidden_units // quarter
    heads_here = HEADS // quarter
    small = fetch_all(qkv_bias, ln1_gain, ln1_bias, ln2_gain, ln2_bias)
    gain_one = small[1].astype(jnp.float32)
    shift_one = small[2].astype(jnp.float32)
    gain_two = small[3].astype(jnp.float32)
    shift_two = small[4].astype(jnp.float32)
    bias_here = (
        lax.dynamic_slice_in_dim(small[0].reshape(3, width), seq_spot * width_part, width_part, 1)
        .astype(jnp.float32)
        .reshape(3 * width_part)
    )

    def attn_blocks():
        return fetch_block(
            qkv_weight.reshape(own_rows, 3, width), out_weight.reshape(own_rows, 1, width)
        )

    def mlp_blocks():
        return fetch_block(
            jnp.stack([gate_weight, up_weight], axis=1),
            down_weight.reshape(own_rows, 1, hidden_units),
        )

    attn_fwd = attn_blocks()
    qkv_block = attn_fwd[0].reshape(width, 3 * width_part)
    out_block = attn_fwd[1].reshape(width, width_part)
    inputs = layer_input.astype(jnp.float32)
    normed_low = layer_norm(inputs, gain_one, shift_one).astype(jnp.bfloat16)
    normed_all = seq_rows(normed_low)
    length = normed_all.shape[0]
    mixed = jnp.dot(normed_all, qkv_block, preferred_element_type=jnp.float32) + bias_here
    cosine, sine = rotary_tables(positions)
    query_low = rotate(
        mixed[:, :width_part].reshape(length, heads_here, HEAD_DIM), cosine, sine
    ).astype(jnp.bfloat16)
    key_low = rotate(
        mixed[:, width_part : 2 * width_part].reshape(length, heads_here, HEAD_DIM), cosine, sine
    ).astype(jnp.bfloat16)
    value_low = (
        mixed[:, 2 * width_part :].reshape(length, heads_here, HEAD_DIM).astype(jnp.bfloat16)
    )
    segment_row = segment_ids[0]
    index = jnp.arange(length)

    def block_scores():
        scores = (
            jnp.einsum("thd,lhd->htl", query_low, key_low, preferred_element_type=jnp.float32)
            * 0.125
        )
        allowed = (segment_row[:, None] == segment_row[None, :]) & (
            index[None, :] <= index[:, None]
        )
        return jnp.where(allowed[None], scores, -1e30)

    scores = block_scores()
    top = jnp.max(scores, axis=-1, keepdims=True)
    expo = jnp.exp(scores - top)
    total = jnp.sum(expo, axis=-1, keepdims=True)
    probs = (expo / total).astype(jnp.bfloat16)
    log_sums = top + jnp.log(total)
    pieces = jnp.einsum("htl,lhd->thd", probs, value_low, preferred_element_type=jnp.float32)
    attended_low = pieces.reshape(length, width_part).astype(jnp.bfloat16)
    hidden = inputs + seq_sums(contract_cols(attended_low, out_block))
    mlp_fwd = mlp_blocks()
    pair_block = mlp_fwd[0].reshape(width, 2 * units_part)
    down_block = mlp_fwd[1].reshape(width, units_part)
    normed2_low = layer_norm(hidden, gain_two, shift_two).astype(jnp.bfloat16)
    normed2_all = seq_rows(normed2_low)
    gate_up = jnp.dot(normed2_all, pair_block, preferred_element_type=jnp.float32)
    gate = gate_up[:, :units_part]
    up = gate_up[:, units_part:]
    inner_low = swiglu(gate, up).astype(jnp.bfloat16)
    result = hidden + seq_sums(contract_cols(inner_low, down_block))
    mlp_back = mlp_blocks()
    pair_back = mlp_back[0].reshape(width, 2 * units_part)
    down_back = mlp_back[1].reshape(width, units_part)
    cotangent_all = seq_rows(cotangent)
    inner_grad = jnp.dot(cotangent_all, down_back, preferred_element_type=jnp.float32)
    down_grad = contract_rows(cotangent_all, inner_low)
    unused, pull_swiglu = jax.vjp(swiglu, gate, up)
    gate_grad, up_grad = pull_swiglu(inner_grad)
    pair_low = jnp.concatenate(
        [gate_grad.astype(jnp.bfloat16), up_grad.astype(jnp.bfloat16)], axis=1
    )
    pair_wgrad = contract_rows(normed2_all, pair_low)
    normed2_grad = seq_sums(contract_cols(pair_low, pair_back))
    unused_two, pull_norm_two = jax.vjp(layer_norm, hidden, gain_two, shift_two)
    hidden_part, gain_two_grad, shift_two_grad = pull_norm_two(normed2_grad)
    hidden_grad = cotangent.astype(jnp.float32) + hidden_part
    mlp_shares = return_block(
        pair_wgrad.reshape(width, 2, units_part), down_grad.reshape(width, 1, units_part)
    )
    attn_back = attn_blocks()
    qkv_back = attn_back[0].reshape(width, 3 * width_part)
    out_back = attn_back[1].reshape(width, width_part)
    branch_all = seq_rows(hidden_grad.astype(jnp.bfloat16))
    out_wgrad = contract_rows(branch_all, attended_low)
    attended_grad = (
        jnp.dot(branch_all, out_back, preferred_element_type=jnp.float32)
        .astype(jnp.bfloat16)
        .reshape(length, heads_here, HEAD_DIM)
    )
    scores = block_scores()
    probs = jnp.exp(scores - log_sums)
    probs_low = probs.astype(jnp.bfloat16)
    value_grad = jnp.einsum(
        "htl,thd->lhd", probs_low, attended_grad, preferred_element_type=jnp.float32
    )
    probs_grad = jnp.einsum(
        "thd,lhd->htl", attended_grad, value_low, preferred_element_type=jnp.float32
    )
    center = jnp.sum(probs * probs_grad, axis=-1, keepdims=True)
    scores_low = (probs * (probs_grad - center)).astype(jnp.bfloat16)
    query_pieces = (
        jnp.einsum("htl,lhd->thd", scores_low, key_low, preferred_element_type=jnp.float32) * 0.125
    )
    key_grad = (
        jnp.einsum("htl,thd->lhd", scores_low, query_low, preferred_element_type=jnp.float32)
        * 0.125
    )
    query_back = rotate(query_pieces, cosine, -sine).reshape(length, width_part)
    key_back = rotate(key_grad, cosine, -sine).reshape(length, width_part)
    mixed_low = jnp.concatenate(
        [query_back, key_back, value_grad.reshape(length, width_part)], axis=1
    ).astype(jnp.bfloat16)
    qkv_wgrad = contract_rows(normed_all, mixed_low)
    bias_part = jnp.sum(mixed_low.astype(jnp.float32), axis=0).reshape(3, width_part)
    slot_mask = (jnp.arange(quarter) == seq_spot).astype(jnp.float32)
    bias_whole = (bias_part[:, None, :] * slot_mask[None, :, None]).reshape(3 * width)
    normed_grad = seq_sums(contract_cols(mixed_low, qkv_back))
    unused_one, pull_norm_one = jax.vjp(layer_norm, inputs, gain_one, shift_one)
    input_part, gain_one_grad, shift_one_grad = pull_norm_one(normed_grad)
    input_grad = hidden_grad + input_part
    attn_shares = return_block(
        qkv_wgrad.reshape(width, 3, width_part), out_wgrad.reshape(width, 1, width_part)
    )
    small_shares = sum_all(bias_whole, gain_one_grad, shift_one_grad, gain_two_grad, shift_two_grad)
    gate_wgrad = mlp_shares[0][:, 0, :]
    up_wgrad = mlp_shares[0][:, 1, :]
    down_wgrad = mlp_shares[1].reshape(own_rows, hidden_units)
    qkv_share = attn_shares[0].reshape(own_rows, 3 * width)
    out_share = attn_shares[1].reshape(own_rows, width)
    return (
        result.astype(jnp.bfloat16),
        input_grad,
        small_shares[1],
        small_shares[2],
        qkv_share,
        small_shares[0],
        out_share,
        small_shares[3],
        small_shares[4],
        gate_wgrad,
        up_wgrad,
        down_wgrad,
    )


def body(
    layer_input,
    segment_ids,
    positions,
    ln1_gain,
    ln1_bias,
    qkv_weight,
    qkv_bias,
    out_weight,
    ln2_gain,
    ln2_bias,
    gate_weight,
    up_weight,
    down_weight,
    cotangent,
):
    return split_heads(
        layer_input,
        segment_ids,
        positions,
        ln1_gain,
        ln1_bias,
        qkv_weight,
        qkv_bias,
        out_weight,
        ln2_gain,
        ln2_bias,
        gate_weight,
        up_weight,
        down_weight,
        cotangent,
    )


def solution(mesh):
    placed = (
        P(("fsdp", "seq"), None),
        P("fsdp", None),
        P("fsdp"),
        P(("fsdp", "seq")),
        P(("fsdp", "seq")),
        P(("fsdp", "seq"), None),
        P(("fsdp", "seq")),
        P(("fsdp", "seq"), None),
        P(("fsdp", "seq")),
        P(("fsdp", "seq")),
        P(("fsdp", "seq"), None),
        P(("fsdp", "seq"), None),
        P(("fsdp", "seq"), None),
        P(("fsdp", "seq"), None),
    )
    return jax.shard_map(
        body,
        mesh=mesh,
        in_specs=placed,
        out_specs=(
            P(("fsdp", "seq"), None),
            P(("fsdp", "seq"), None),
            P(("fsdp", "seq")),
            P(("fsdp", "seq")),
            P(("fsdp", "seq"), None),
            P(("fsdp", "seq")),
            P(("fsdp", "seq"), None),
            P(("fsdp", "seq")),
            P(("fsdp", "seq")),
            P(("fsdp", "seq"), None),
            P(("fsdp", "seq"), None),
            P(("fsdp", "seq"), None),
        ),
        check_vma=False,
    )
```

profile of v0, /device:TPU:0, one launch (start us, length us, event | category | flops | bytes accessed | tf_op | source)
XLA Modules:
  0.0 2342.5 jit_solution(12369615966745718935)
XLA Ops:
  7.2 2.7 reshape.307
  13.2 15.8 all_to_all.155
  29.0 3.0 reshape.342
  35.5 43.4 %all-reduce.15 = (bf16[2048]{0:T(1024)(128)(2,1)S(1)}, bf16[2048]{0:T(1024)(128)(2,1)S(1)}, bf16[3,2048]{1,0:T(4,128)(2,1)S(1)}, bf16[2048]{0:T(1024)(128)(2,1)}, bf16[2048]{0:T(1024)(128)(2,1)}) all-reduce(bf16[2048]{0:T(1024)(128)(2,1)S(1)} %dynamic-update-slice.1, ...), channel_id=1, replica_groups=mesh['fsdp'=8,'seq'=4] {'fsdp','seq'}, use_global_device_ids=true, to_apply=%add.1 | all-reduce | flops 14336 | bytes 57344
  82.4 11.5 reduce
  95.1 3.5 all-to-all-start.1
  100.8 3.9 all-to-all-done.1
  106.9 28.3 %all-gather.11.cloned.1.call-done = bf16[2048,3,512]{2,0,1:T(8,128)(2,1)} async-done(((bf16[256,3,512]{2,0,1:T(8,128)(2,1)}), bf16[2048,3,512]{2,0,1:T(8,128)(2,1)}) %all-gather.11.cloned.1.call-update) | async-done | bytes 6291472 | tf_op jit(solution)/shard_map/all_gather | solution.py:76
  135.2 8.9 copy.138
  144.2 14.0 all-gather.9.cloned.1.call-done
  158.2 6.2 convolution_add_fusion
  171.1 2.6 fusion.57
  178.6 31.6 %all-gather.13.cloned.1.call-done = bf16[2048,1,512]{2,0,1:T(8,128)(2,1)} async-done(((bf16[256,1,512]{2,0,1:T(8,128)(2,1)}), bf16[2048,1,512]{2,0,1:T(8,128)(2,1)}) %all-gather.13.cloned.1.call-update) | async-done | bytes 2097168 | tf_op jit(solution)/shard_map/all_gather | solution.py:77
  210.2 4.9 fusion.16
  217.6 6.4 copy.146
  224.0 3.2 reshape.345
  227.2 38.5 %all_to_all.156 = bf16[4,2,90112]{2,1,0:T(2,128)(2,1)} all-to-all(bf16[4,2,90112]{2,1,0:T(2,128)(2,1)} %reshape.345), channel_id=1, replica_groups=mesh['fsdp'=8,'seq'=4] {'seq'}, dimensions={0} | all-to-all | bytes 2883584 | tf_op jit(solution)/shard_map/all_to_all | solution.py:72
  265.6 3.6 reshape.346
  269.2 5.0 copy.170
  274.3 2.6 copy.148
  280.7 4.8 copy.150
  285.5 31.6 %reduce.1 = bf16[5632,64]{1,0:T(8,128)(2,1)S(1)} reduce(bf16[5632,1,64]{2,1,0:T(2,128)(2,1)} %bitcast.128, bf16[]{:T(256)} %broadcast.232), dimensions={1}, to_apply=%bitcast.94.reduce_sub_computation | reduce | bytes 1441794
  319.5 14.4 all_to_all.157
  333.9 2.6 reshape.348
  336.5 6.0 copy.151
  343.9 94.4 %all-gather.17.cloned.1.call-done = bf16[2048,2,1408]{2,0,1:T(8,128)(2,1)} async-done(((bf16[256,2,1408]{2,0,1:T(8,128)(2,1)}), bf16[2048,2,1408]{2,0,1:T(8,128)(2,1)}) %all-gather.17.cloned.1.call-update) | async-done | bytes 11534352 | tf_op jit(solution)/shard_map/all_gather | solution.py:76
  438.4 15.4 copy.149
  453.8 7.4 all-gather.15.cloned.1.call-done
  461.2 12.6 fusion.58
  473.8 11.7 all-gather.21.cloned.1.call-done
  485.5 95.7 %all-gather.19.cloned.1.call-done = bf16[2048,1,1408]{2,0,1:T(8,128)(2,1)} async-done(((bf16[256,1,1408]{2,0,1:T(8,128)(2,1)}), bf16[2048,1,1408]{2,0,1:T(8,128)(2,1)}) %all-gather.19.cloned.1.call-update) | async-done | bytes 5767184 | tf_op jit(solution)/shard_map/all_gather | solution.py:77
  581.1 9.4 fusion.12
  592.1 7.6 fusion.19
  599.8 7.7 fusion.4
  607.6 35.0 %reduce-scatter.11.cloned.1.call-done = f32[128,2048]{1,0:T(8,128)} async-done(((f32[512,2048]{1,0:T(8,128)}), f32[128,2048]{1,0:T(8,128)}) %reduce-scatter.11.cloned.1.call-update) | async-done | bytes 1048592 | tf_op jit(solution)/shard_map/reduce_scatter | solution.py:97
  644.2 45.3 %reduce-scatter.9.cloned.1.call-done = f32[128,2048]{1,0:T(8,128)} async-done(((f32[512,2048]{1,0:T(8,128)}), f32[128,2048]{1,0:T(8,128)}) %reduce-scatter.9.cloned.1.call-update) | async-done | bytes 1048592 | tf_op jit(solution)/shard_map/reduce_scatter | solution.py:97
  689.5 2.7 fusion.54
  694.6 22.3 all-gather.23.cloned.1.call-done
  716.9 4.9 convolution_bitcast_fusion.1
  723.4 7.4 convolution_bitcast_fusion
  732.4 12.8 fusion.18
  745.2 26.9 %reshape.325 = f32[2048,2,1408]{2,1,0:T(2,128)} reshape(f32[2048,2816]{1,0:T(8,128)} %fusion.18) | data formatting | bytes 46137344 | tf_op jit(solution)/shard_map/reshape | solution.py:213
  772.1 3.0 fusion.26
  775.1 5.5 multiply_reduce_fusion
  780.9 2.5 multiply_convert_fusion
  788.0 8.2 fusion.50
  796.3 18.1 copy.156
  814.5 7.8 fusion.51
  824.7 3.5 all-to-all-start.5
  828.2 178.0 %reduce-scatter.17.cloned.1.call-done = f32[256,1,1408]{0,2,1:T(8,128)} async-done(((f32[2048,1,1408]{0,2,1:T(8,128)}), f32[256,1,1408]{0,2,1:T(8,128)}) %reduce-scatter.17.cloned.1.call-update) | async-done | bytes 1441808 | tf_op jit(solution)/shard_map/reduce_scatter | solution.py:84
  1006.2 4.8 copy.162
  1011.7 3.6 all-to-all-start.7
  1016.6 1175.3 %all-reduce.18.cloned.1.call-done = (f32[2048,3,512]{2,1,0:T(4,128)}, f32[2048,2,1408]{2,1,0:T(2,128)}) async-done(((f32[2048,3,512]{2,1,0:T(4,128)}, f32[2048,2,1408]{2,1,0:T(2,128)}), (f32[2048,3,512]{2,1,0:T(4,128)}, f32[2048,2,1408]{2,1,0:T(2,128)})) %all-reduce.18.cloned.1.call-update) | async-done | bytes 35651600
  2191.9 3.3 constant_dynamic-slice_fusion.1
  2196.2 3.7 all-to-all-start.4
  2200.0 5.0 constant_dynamic-slice_fusion
  2205.0 32.4 %all-to-all-done.4 = f32[256,3,512]{2,1,0:T(4,128)S(1)} async-done(((f32[256,3,512]{2,1,0:T(4,128)}), f32[256,3,512]{2,1,0:T(4,128)S(1)}, u32[]{:S(2)}, u32[]{:S(2)}) %all-to-all-start.4) | async-done | bytes 1572896 | tf_op jit(solution)/shard_map/all_to_all | solution.py:87
  2238.8 3.7 all-to-all-start.6
  2244.2 7.6 reduce-scatter.13.cloned.1.call-done
  2255.2 56.4 %all-reduce.13 = (f32[2048]{0:T(1024)S(1)}, f32[2048]{0:T(1024)S(1)}, f32[6144]{0:T(1024)S(1)}, f32[2048]{0:T(1024)S(1)}, f32[2048]{0:T(1024)S(1)}) all-reduce(f32[2048]{0:T(1024)S(1)} %get-tuple-element.14, f32[2048]{0:T(1024)S(1)} %get-tuple-element.17, ...), channel_id=6, replica_groups=mesh['fsdp'=8,'seq'=4] {'fsdp','seq'}, use_global_device_ids=true, to_apply=%region_16.17.clone | all-reduce | flops 14336 | bytes 114688
  2314.6 3.3 add_add_fusion.2
  2324.1 3.2 reshape.322
  2327.4 3.4 copy.161
  2330.8 3.2 all_to_all.143
  (257 shorter events, 73.1 us)
Async XLA Ops:
  7.2 128.1 %all-gather.11.cloned.1.call-start = ((), (), s32[]{:S(2)}) async-start(), calls=%async_computation.15 | async-start | bytes 7077888 | tf_op jit(solution)/shard_map/all_gather | solution.py:76
  28.9 5.3 copy-start.54
  28.9 5.6 copy-start.55
  28.9 5.8 copy-start.56
  29.0 6.1 copy-start.57
  29.0 6.3 copy-start.58
  29.0 49.9 %copy-start.1 = (bf16[128,2048]{1,0:T(8,128)(2,1)S(1)}, bf16[128,2048]{1,0:T(8,128)(2,1)}, u32[]{:S(2)}) copy-start(bf16[128,2048]{1,0:T(8,128)(2,1)} %param.14) | copy-start | bytes 1572868
  32.0 49.2 %copy-start.35 = (bf16[64,2048]{1,0:T(8,128)(2,1)S(1)}, bf16[64,2048]{1,0:T(8,128)(2,1)}, u32[]{:S(2)}) copy-start(bf16[64,2048]{1,0:T(8,128)(2,1)} %param.21) | copy-start | bytes 786436
  34.2 124.0 %all-gather.9.cloned.1.call-start = ((), (), s32[]{:S(2)}) async-start(), calls=%async_computation.14 | async-start | bytes 2621440 | tf_op jit(solution)/shard_map/all_gather | solution.py:93
  79.9 15.2 copy-start.44
  79.9 19.2 copy-start.48
  79.9 19.2 copy-start.43
  95.1 9.6 all-to-all-start.1
  98.6 111.6 %all-gather.13.cloned.1.call-start = ((), (), s32[]{:S(2)}) async-start(), calls=%async_computation.16 | async-start | bytes 2359296 | tf_op jit(solution)/shard_map/all_gather | solution.py:77
  106.8 170.2 %reduce-scatter.7.cloned.1.call-start = ((), (), s32[]{:S(2)}) async-start(), calls=%async_computation.17 | async-start | bytes 5242880 | tf_op jit(solution)/shard_map/reduce_scatter | solution.py:97
  168.0 6.9 copy-start.11
  169.5 4.2 copy-start.20
  169.9 3.8 copy-start.18
  171.1 2.6 copy-start.27
  171.1 2.6 copy-start.29
  171.1 2.6 copy-start.31
  171.1 2.6 copy-start.33
  173.7 3.3 copy-start
  173.8 3.3 copy-start.38
  178.6 36.4 %copy-start.22 = (bf16[8,64,512]{2,1,0:T(8,128)(2,1)}, bf16[8,64,512]{2,1,0:T(8,128)(2,1)S(1)}, u32[]{:S(2)}) copy-start(bf16[8,64,512]{2,1,0:T(8,128)(2,1)S(1)} %fusion.29) | copy-start | bytes 1572868
  215.1 223.2 %all-gather.17.cloned.1.call-start = ((), (), s32[]{:S(2)}) async-start(), calls=%async_computation.19 | async-start | bytes 12976128 | tf_op jit(solution)/shard_map/all_gather | solution.py:76
  274.3 2.7 copy-start.47
  274.3 2.7 copy-start.46
  276.9 184.3 %all-gather.15.cloned.1.call-start = ((), (), s32[]{:S(2)}) async-start(), calls=%async_computation.18 | async-start | bytes 2621440 | tf_op jit(solution)/shard_map/all_gather | solution.py:93
  277.0 3.7 copy-start.24
  279.9 205.6 %all-gather.21.cloned.1.call-start = ((), (), s32[]{:S(2)}) async-start(), calls=%async_computation.22 | async-start | bytes 2621440 | tf_op jit(solution)/shard_map/all_gather | solution.py:93
  280.6 300.5 %all-gather.19.cloned.1.call-start = ((), (), s32[]{:S(2)}) async-start(), calls=%async_computation.20 | async-start | bytes 6488064 | tf_op jit(solution)/shard_map/all_gather | solution.py:77
  343.7 298.9 %reduce-scatter.11.cloned.1.call-start = ((), (), s32[]{:S(2)}) async-start(), calls=%async_computation.23 | async-start | bytes 5242880 | tf_op jit(solution)/shard_map/reduce_scatter | solution.py:97
  581.1 11.0 copy-start.3
  590.5 9.3 copy-start.60
  599.7 89.7 %reduce-scatter.9.cloned.1.call-start = ((), (), s32[]{:S(2)}) async-start(), calls=%async_computation.21 | async-start | bytes 5242880 | tf_op jit(solution)/shard_map/reduce_scatter | solution.py:97
  607.5 109.4 %all-gather.23.cloned.1.call-start = ((), (), s32[]{:S(2)}) async-start(), calls=%async_computation.24 | async-start | bytes 2621440 | tf_op jit(solution)/shard_map/all_gather | solution.py:93
  644.2 48.9 %copy-start.9 = (bf16[128,2048]{1,0:T(8,128)(2,1)S(1)}, bf16[128,2048]{1,0:T(8,128)(2,1)}, u32[]{:S(2)}) copy-start(bf16[128,2048]{1,0:T(8,128)(2,1)} %param.27) | copy-start | bytes 1572868
  644.2 72.7 %copy-start.23 = (bf16[8,64,512]{2,1,0:T(8,128)(2,1)S(1)}, bf16[8,64,512]{2,1,0:T(8,128)(2,1)}, u32[]{:S(2)}) copy-start(bf16[8,64,512]{2,1,0:T(8,128)(2,1)} %copy-done.22) | copy-start | bytes 1572868
  694.2 128.2 %reduce-scatter.15.cloned.1.call-start = ((), (), s32[]{:S(2)}) async-start(), calls=%async_computation.26 | async-start | bytes 4718592 | tf_op jit(solution)/shard_map/reduce_scatter | solution.py:84
  721.8 284.4 %reduce-scatter.17.cloned.1.call-start = ((), (), s32[]{:S(2)}) async-start(), calls=%async_computation.27 | async-start | bytes 12976128 | tf_op jit(solution)/shard_map/reduce_scatter | solution.py:84
  730.8 1461.0 %all-reduce.18.cloned.1.call-start = ((), (), s32[]{:S(2)}) async-start(), calls=%async_computation.28 | async-start | bytes 79691776
  745.2 26.9 %copy-start.17 = (bf16[2048,1,512]{2,0,1:T(8,128)(2,1)S(1)}, bf16[2048,1,512]{2,0,1:T(8,128)(2,1)}, u32[]{:S(2)}) copy-start(bf16[2048,1,512]{2,0,1:T(8,128)(2,1)} %all-gather.13.cloned.1.call-done) | copy-start | bytes 6291460
  772.1 3.0 copy-start.12
  775.0 5.5 slice-start
  775.1 5.9 slice-start.1
  780.9 2.6 copy-start.32
  780.9 2.6 copy-start.34
  786.1 28.4 %copy-start.15 = (bf16[512,8,64]{0,2,1:T(8,128)(2,1)}, bf16[512,8,64]{0,2,1:T(8,128)(2,1)S(1)}, u32[]{:S(2)}) copy-start(bf16[512,8,64]{0,2,1:T(8,128)(2,1)S(1)} %get-tuple-element.62) | copy-start | bytes 1572868
  786.1 28.4 %copy-start.16 = (bf16[512,8,64]{0,2,1:T(8,128)(2,1)}, bf16[512,8,64]{0,2,1:T(8,128)(2,1)S(1)}, u32[]{:S(2)}) copy-start(bf16[512,8,64]{0,2,1:T(8,128)(2,1)S(1)} %get-tuple-element.63) | copy-start | bytes 1572868
  787.5 27.0 %copy-start.10 = (bf16[8,64,512]{2,1,0:T(8,128)(2,1)}, bf16[8,64,512]{2,1,0:T(8,128)(2,1)S(1)}, u32[]{:S(2)}) copy-start(bf16[8,64,512]{2,1,0:T(8,128)(2,1)S(1)} %fusion.30) | copy-start | bytes 1572868
  814.4 1437.5 %reduce-scatter.13.cloned.1.call-start = ((), (), s32[]{:S(2)}) async-start(), calls=%async_computation.25 | async-start | bytes 5242880 | tf_op jit(solution)/shard_map/reduce_scatter | solution.py:97
  824.7 186.3 %all-to-all-start.5 = ((f32[256,1,512]{2,1,0:T(1,128)}), f32[256,1,512]{2,1,0:T(1,128)S(1)}, u32[]{:S(2)}, u32[]{:S(2)}) async-start(f32[256,1,512]{2,1,0:T(1,128)} %copy.159), calls=%async_computation.10 | async-start | bytes 1048576 | tf_op jit(solution)/shard_map/all_to_all | solution.py:88
  828.2 187.1 %copy-start.59 = (u32[32]{0:T(128)S(1)}, u32[32]{0:T(128)}, u32[]{:S(2)}) copy-start(u32[32]{0:T(128)} %constant.71) | copy-start | bytes 388
  1011.7 1183.4 %all-to-all-start.7 = ((f32[256,1,1408]{2,1,0:T(1,128)}), f32[256,1,1408]{2,1,0:T(1,128)S(1)}, u32[]{:S(2)}, u32[]{:S(2)}) async-start(f32[256,1,1408]{2,1,0:T(1,128)} %copy.162), calls=%async_computation.13 | async-start | bytes 2883584 | tf_op jit(solution)/shard_map/all_to_all | solution.py:88
  2196.2 41.2 %all-to-all-start.4 = ((f32[256,3,512]{2,1,0:T(4,128)}), f32[256,3,512]{2,1,0:T(4,128)S(1)}, u32[]{:S(2)}, u32[]{:S(2)}) async-start(f32[256,3,512]{2,1,0:T(4,128)} %constant_dynamic-slice_fusion.1), calls=%async_computation.8 | async-start | bytes 4194304 | tf_op jit(solution)/shard_map/all_to_all | solution.py:87
  2205.0 46.9 %copy-start.2 = (bf16[128,2048]{1,0:T(8,128)(2,1)S(1)}, bf16[128,2048]{1,0:T(8,128)(2,1)}, u32[]{:S(2)}) copy-start(bf16[128,2048]{1,0:T(8,128)(2,1)} %param.14) | copy-start | bytes 1572868
  2205.0 46.9 %copy-start.37 = (f32[2048]{0:T(1024)S(1)}, f32[2048]{0:T(1024)}, u32[]{:S(2)}) copy-start(f32[2048]{0:T(1024)} %copy-done.36) | copy-start | bytes 24580
  2205.0 46.9 %copy-start.42 = (f32[128]{0:T(128)S(1)}, f32[128]{0:T(128)}, u32[]{:S(2)}) copy-start(f32[128]{0:T(128)} %copy-done.41) | copy-start | bytes 1540
  2238.8 88.6 %all-to-all-start.6 = ((f32[256,2,1408]{2,1,0:T(2,128)}), f32[256,2,1408]{2,1,0:T(2,128)S(1)}, u32[]{:S(2)}, u32[]{:S(2)}) async-start(f32[256,2,1408]{2,1,0:T(2,128)} %constant_dynamic-slice_fusion), calls=%async_computation.11 | async-start | bytes 5767168 | tf_op jit(solution)/shard_map/all_to_all | solution.py:87
  2242.4 11.0 copy-start.50
  2242.4 11.0 copy-start.45
  2311.6 6.3 copy-start.14
  2314.6 4.6 copy-start.8
  (21 other events, 30.0 us)
Sparse Core Ops, SparseCore 0:
  34.3 100.9 all-gather.10
  137.4 20.7 all-gather.8
  160.9 49.2 all-gather.12
  215.2 58.4 reduce-scatter.6
  277.1 161.2 all-gather.16
  440.4 20.7 all-gather.14
  462.8 22.5 all-gather.20
  488.5 92.6 all-gather.18
  599.9 42.6 reduce-scatter.10
  644.9 44.4 reduce-scatter.8
  694.3 22.5 all-gather.22
  721.9 87.9 reduce-scatter.14
  813.5 192.6 reduce-scatter.16
  1010.5 1181.3 all-reduce.17
  2194.2 57.5 reduce-scatter.12
where the time goes:
time: 2350 us; the launch traced here: 2340 us
  waiting for transfers between devices  1780 us (76%)
  local copies, waits for them, and re-layouts  180 us (8%)
  blocking collectives  168 us (7%)
  matrix products  106 us (5%)
  other arithmetic  69.2 us (3%)
    unnamed x16, waiting for transfers between devices  1180 us
    reduce_scatter x2, waiting for transfers between devices, return_block(): lax.psum_scatter(second, 'fsdp', scatter_dimension=0, tiled=True)  178 us
    all_gather x2, waiting for transfers between devices, fetch_block(): lax.all_gather(columns[1], 'fsdp', axis=0, tiled=True)  127 us
    all_gather x2, waiting for transfers between devices, fetch_block(): lax.all_gather(columns[0], 'fsdp', axis=0, tiled=True)  123 us
    unnamed x2, blocking collectives  99.8 us
    reduce_scatter x4, waiting for transfers between devices, seq_sums(): return lax.psum_scatter(values, 'seq', scatter_dimension=0, tiled=True)  87.9 us
    all_gather x4, waiting for transfers between devices, seq_rows(): return lax.all_gather(values, 'seq', axis=0, tiled=True)  55.4 us
    all_to_all x2, blocking collectives, fetch_block(): lax.all_to_all(first, 'seq', split_axis=2, concat_axis=0, tiled=True)  54.2 us
  transfers between devices with their start and end apart: 20, of which 15 were waited for; matrix products, arithmetic and copies ran while one was open for 12% of the time, Pallas kernels for 0%

commit v1 on v0

--- a/solution.py
+++ b/solution.py
@@ -5,6 +5,34 @@
 
 HEADS = 32
 HEAD_DIM = 64
+
+
+def _place_page(q_in):
+    piece_out, v_now, mat_out = (lax.axis_size("seq"), lax.axis_index("seq"), q_in.shape[0])
+    pool = [p * piece_out if dev_i == 0 else p for dev_i, p in enumerate(q_in.shape)]
+    tile_out = later = q_in
+    x_now = lax.dynamic_update_slice_in_dim(
+        jnp.zeros(pool, q_in.dtype), q_in, v_now * mat_out, axis=0
+    )
+    for j0 in range(1, piece_out // 2 + 1):
+        tile_out = lax.ppermute(
+            tile_out,
+            "seq",
+            list(map(lambda dev_i: (dev_i, (dev_i + 1) % piece_out), range(piece_out))),
+        )
+        x_now = lax.dynamic_update_slice_in_dim(
+            x_now, tile_out, (v_now - j0) % piece_out * mat_out, axis=0
+        )
+        if 2 * j0 < piece_out:
+            later = lax.ppermute(
+                later,
+                "seq",
+                list(map(lambda dev_i: (dev_i, (dev_i - 1) % piece_out), range(piece_out))),
+            )
+            x_now = lax.dynamic_update_slice_in_dim(
+                x_now, later, (v_now + j0) % piece_out * mat_out, axis=0
+            )
+    return x_now
 
 
 def layer_norm(values, gain, shift):
@@ -90,7 +118,7 @@
 
 
 def seq_rows(values):
-    return lax.all_gather(values, "seq", axis=0, tiled=True)
+    return _place_page(values)
 
 
 def seq_sums(values):

time: 2350 us -> 2280 us (0.970)
  waiting for transfers between devices: 1780 us -> 1690 us
    all_gather x4 -> x0, waiting for transfers between devices: 55.4 us -> none  [seq_rows(): return lax.all_gather(values, 'seq', axis=0, tiled=True)]
    all_gather x2, waiting for transfers between devices: 123 us -> 77.7 us  [fetch_block(): lax.all_gather(columns[0], 'fsdp', axis=0, tiled=True)]
    ppermute x0 -> x12, waiting for transfers between devices: none -> 43.7 us  [the longest x8 43.7 us: _place_page(): lax.ppermute(tile_out, 'seq', list(map(lambda dev_i: (dev_i, (dev_i + 1)...]
    all_gather x2, waiting for transfers between devices: 127 us -> 87.4 us  [fetch_block(): lax.all_gather(columns[1], 'fsdp', axis=0, tiled=True)]
    unnamed x16 -> x12, waiting for transfers between devices: 1180 us -> 1180 us
    unnamed x161 -> x162, local copies, waits for them, and re-layouts: 47.5 us -> 47.6 us
  transfers between devices with their start and end apart: 20 -> 28, of which waited for: 15 -> 17; matrix products, arithmetic and copies ran while one was open for 12% -> 13% of each run, Pallas kernels for 0% -> 0%
where the time goes in v1:
time: 2280 us; the launch traced here: 2270 us
  waiting for transfers between devices  1690 us (74%)
  local copies, waits for them, and re-layouts  196 us (9%)
  blocking collectives  168 us (7%)
  matrix products  106 us (5%)
  other arithmetic  67.7 us (3%)
  starting transfers between devices  27.3 us (1%)
    unnamed x12, waiting for transfers between devices  1180 us
    reduce_scatter x2, waiting for transfers between devices, return_block(): lax.psum_scatter(second, 'fsdp', scatter_dimension=0, tiled=True)  178 us
    unnamed x2, blocking collectives  99.8 us
    all_gather x2, waiting for transfers between devices, fetch_block(): lax.all_gather(columns[1], 'fsdp', axis=0, tiled=True)  87.4 us
    reduce_scatter x4, waiting for transfers between devices, seq_sums(): return lax.psum_scatter(values, 'seq', scatter_dimension=0, tiled=True)  87.2 us
    all_gather x2, waiting for transfers between devices, fetch_block(): lax.all_gather(columns[0], 'fsdp', axis=0, tiled=True)  77.7 us
    all_to_all x2, blocking collectives, fetch_block(): lax.all_to_all(first, 'seq', split_axis=2, concat_axis=0, tiled=True)  54.2 us
    unnamed x162, local copies, waits for them, and re-layouts  47.6 us
  transfers between devices with their start and end apart: 28, of which 17 were waited for; matrix products, arithmetic and copies ran while one was open for 13% of the time, Pallas kernels for 0%

profile of v1, /device:TPU:0, one launch (start us, length us, event | category | flops | bytes accessed | tf_op | source)
XLA Modules:
  0.0 2266.7 jit_solution(17646020488042857118)
XLA Ops:
  7.2 2.7 reshape.307
  13.2 15.8 all_to_all.155
  29.0 3.0 reshape.342
  35.5 43.4 %all-reduce.15 = (bf16[2048]{0:T(1024)(128)(2,1)S(1)}, bf16[2048]{0:T(1024)(128)(2,1)S(1)}, bf16[3,2048]{1,0:T(4,128)(2,1)S(1)}, bf16[2048]{0:T(1024)(128)(2,1)}, bf16[2048]{0:T(1024)(128)(2,1)}) all-reduce(bf16[2048]{0:T(1024)(128)(2,1)S(1)} %dynamic-update-slice.1, ...), channel_id=1, replica_groups=mesh['fsdp'=8,'seq'=4] {'fsdp','seq'}, use_global_device_ids=true, to_apply=%add.1 | all-reduce | flops 14336 | bytes 57344
  83.2 11.5 reduce
  95.8 3.5 all-to-all-start.1
  102.1 3.8 all-to-all-done.1
  113.0 22.2 all-gather.5.cloned.1.call-done
  135.2 8.8 copy.137
  144.0 5.7 convolution_add_fusion
  163.9 21.7 all-gather.7.cloned.1.call-done
  185.6 4.9 fusion.16
  193.0 6.4 copy.145
  199.4 3.2 reshape.345
  202.5 38.4 %all_to_all.156 = bf16[4,2,90112]{2,1,0:T(2,128)(2,1)} all-to-all(bf16[4,2,90112]{2,1,0:T(2,128)(2,1)} %reshape.345), channel_id=1, replica_groups=mesh['fsdp'=8,'seq'=4] {'seq'}, dimensions={0} | all-to-all | bytes 2883584 | tf_op jit(solution)/shard_map/all_to_all | solution.py:100
  240.9 3.6 reshape.346
  244.6 5.0 copy.169
  249.6 2.6 copy.147
  252.5 6.1 copy.149
  258.5 31.7 %reduce.1 = bf16[5632,64]{1,0:T(8,128)(2,1)} reduce(bf16[5632,1,64]{2,1,0:T(2,128)(2,1)S(1)} %bitcast.126, bf16[]{:T(256)} %broadcast.239), dimensions={1}, to_apply=%bitcast.92.reduce_sub_computation | reduce | bytes 1441794
  290.2 3.0 reshape.347
  293.2 14.1 all_to_all.157
  307.3 2.7 reshape.348
  310.0 4.5 copy.150
  319.3 12.0 collective-permute-done.6
  342.6 5.9 collective-permute-done.3
  351.2 6.1 collective-permute-done.5
  358.2 55.5 %all-gather.9.cloned.1.call-done = bf16[2048,2,1408]{2,0,1:T(8,128)(2,1)} async-done(((bf16[256,2,1408]{2,0,1:T(8,128)(2,1)}), bf16[2048,2,1408]{2,0,1:T(8,128)(2,1)}) %all-gather.9.cloned.1.call-update) | async-done | bytes 11534352 | tf_op jit(solution)/shard_map/all_gather | solution.py:104
  413.7 15.3 copy.148
  428.9 12.7 fusion.61
  441.6 65.8 %all-gather.11.cloned.1.call-done = bf16[2048,1,1408]{2,0,1:T(8,128)(2,1)} async-done(((bf16[256,1,1408]{2,0,1:T(8,128)(2,1)}), bf16[2048,1,1408]{2,0,1:T(8,128)(2,1)}) %all-gather.11.cloned.1.call-update) | async-done | bytes 5767184 | tf_op jit(solution)/shard_map/all_gather | solution.py:105
  507.4 10.5 fusion.12
  519.4 7.6 fusion.19
  527.1 8.6 fusion.4
  535.8 34.1 %reduce-scatter.11.cloned.1.call-done = f32[128,2048]{1,0:T(8,128)} async-done(((f32[512,2048]{1,0:T(8,128)}), f32[128,2048]{1,0:T(8,128)}) %reduce-scatter.11.cloned.1.call-update) | async-done | bytes 1048592 | tf_op jit(solution)/shard_map/reduce_scatter | solution.py:125
  571.5 45.4 %reduce-scatter.9.cloned.1.call-done = f32[128,2048]{1,0:T(8,128)} async-done(((f32[512,2048]{1,0:T(8,128)}), f32[128,2048]{1,0:T(8,128)}) %reduce-scatter.9.cloned.1.call-update) | async-done | bytes 1048592 | tf_op jit(solution)/shard_map/reduce_scatter | solution.py:125
  616.9 2.7 fusion.56
  622.3 11.0 collective-permute-done.9
  633.5 8.5 collective-permute-done.11
  643.4 3.3 convolution_bitcast_fusion.1
  648.0 7.8 convolution_bitcast_fusion
  657.2 12.7 fusion.18
  669.9 26.9 %reshape.325 = f32[2048,2,1408]{2,1,0:T(2,128)} reshape(f32[2048,2816]{1,0:T(8,128)} %fusion.18) | data formatting | bytes 46137344 | tf_op jit(solution)/shard_map/reshape | solution.py:241
  696.8 3.0 fusion.26
  699.8 5.5 multiply_reduce_fusion
  712.8 8.2 fusion.51
  721.0 18.1 copy.155
  739.2 7.8 fusion.52
  749.4 3.5 all-to-all-start.5
  752.9 177.6 %reduce-scatter.17.cloned.1.call-done = f32[256,1,1408]{2,0,1:T(8,128)} async-done(((f32[2048,1,1408]{2,0,1:T(8,128)}), f32[256,1,1408]{2,0,1:T(8,128)}) %reduce-scatter.17.cloned.1.call-update) | async-done | bytes 1441808 | tf_op jit(solution)/shard_map/reduce_scatter | solution.py:112
  930.6 3.9 copy.161
  935.3 3.6 all-to-all-start.7
  940.1 1176.1 %all-reduce.18.cloned.1.call-done = (f32[2048,3,512]{2,1,0:T(4,128)}, f32[2048,2,1408]{2,1,0:T(2,128)}) async-done(((f32[2048,3,512]{2,1,0:T(4,128)}, f32[2048,2,1408]{2,1,0:T(2,128)}), (f32[2048,3,512]{2,1,0:T(4,128)}, f32[2048,2,1408]{2,1,0:T(2,128)})) %all-reduce.18.cloned.1.call-update) | async-done | bytes 35651600
  2116.2 3.3 constant_dynamic-slice_fusion.2
  2120.6 3.8 all-to-all-start.4
  2124.4 5.0 constant_dynamic-slice_fusion.1
  2129.3 32.4 %all-to-all-done.4 = f32[256,3,512]{2,1,0:T(4,128)S(1)} async-done(((f32[256,3,512]{2,1,0:T(4,128)}), f32[256,3,512]{2,1,0:T(4,128)S(1)}, u32[]{:S(2)}, u32[]{:S(2)}) %all-to-all-start.4) | async-done | bytes 1572896 | tf_op jit(solution)/shard_map/all_to_all | solution.py:115
  2163.1 3.7 all-to-all-start.6
  2168.6 7.7 reduce-scatter.13.cloned.1.call-done
  2179.6 56.4 %all-reduce.13 = (f32[2048]{0:T(1024)S(1)}, f32[2048]{0:T(1024)S(1)}, f32[6144]{0:T(1024)S(1)}, f32[2048]{0:T(1024)S(1)}, f32[2048]{0:T(1024)S(1)}) all-reduce(f32[2048]{0:T(1024)S(1)} %get-tuple-element.14, f32[2048]{0:T(1024)S(1)} %get-tuple-element.17, ...), channel_id=6, replica_groups=mesh['fsdp'=8,'seq'=4] {'fsdp','seq'}, use_global_device_ids=true, to_apply=%region_16.17.clone | all-reduce | flops 14336 | bytes 114688
  2238.9 3.3 add_add_fusion.2
  2248.4 3.2 reshape.322
  2251.6 3.4 copy.160
  2255.0 3.2 all_to_all.143
  (287 shorter events, 97.8 us)
Async XLA Ops:
  7.2 128.0 %all-gather.5.cloned.1.call-start = ((), (), s32[]{:S(2)}) async-start(), calls=%async_computation.14 | async-start | bytes 7077888 | tf_op jit(solution)/shard_map/all_gather | solution.py:104
  28.9 5.2 copy-start.54
  28.9 5.5 copy-start.55
  28.9 5.8 copy-start.56
  28.9 6.0 copy-start.57
  29.0 6.3 copy-start.58
  29.0 49.9 %copy-start.1 = (bf16[128,2048]{1,0:T(8,128)(2,1)S(1)}, bf16[128,2048]{1,0:T(8,128)(2,1)}, u32[]{:S(2)}) copy-start(bf16[128,2048]{1,0:T(8,128)(2,1)} %param.14) | copy-start | bytes 1572868
  34.1 47.8 %copy-start.38 = (bf16[64,2048]{1,0:T(8,128)(2,1)S(1)}, bf16[64,2048]{1,0:T(8,128)(2,1)}, u32[]{:S(2)}) copy-start(bf16[64,2048]{1,0:T(8,128)(2,1)} %param.21) | copy-start | bytes 786436
  78.9 3.8 copy-start.39
  79.0 3.6 copy-start.44
  79.6 20.2 copy-start.51
  79.6 20.2 copy-start.46
  80.1 21.5 collective-permute-start
  80.1 28.9 %collective-permute-start.1 = (bf16[128,2048]{1,0:T(8,128)(2,1)S(1)}, bf16[128,2048]{1,0:T(8,128)(2,1)}, u32[]{:S(2)}, u32[]{:S(2)}) collective-permute-start(bf16[128,2048]{1,0:T(8,128)(2,1)S(1)} %get-tuple-element.40), channel_id=1, source_target_pairs={{0,3},{1,0},{2,1},{3,2},{4,7},{5,4},{6,5},{7,6},{8,11},{9,8},{10,9... | collective-permute-start | bytes 1572872 | tf_op jit(solution)/shard_map/ppermute | solution.py:27
  95.8 10.2 all-to-all-start.1
  99.4 86.2 %all-gather.7.cloned.1.call-start = ((), (), s32[]{:S(2)}) async-start(), calls=%async_computation.15 | async-start | bytes 2359296 | tf_op jit(solution)/shard_map/all_gather | solution.py:105
  101.5 53.6 %copy-start.41 = (f32[512,8]{0,1:T(8,128)}, f32[512,8]{0,1:T(8,128)S(1)}, u32[]{:S(2)}) copy-start(f32[512,8]{0,1:T(8,128)S(1)} %get-tuple-element.63) | copy-start | bytes 49156
  101.5 9.6 collective-permute-start.2
  108.2 223.2 %reduce-scatter.7.cloned.1.call-start = ((), (), s32[]{:S(2)}) async-start(), calls=%async_computation.16 | async-start | bytes 5242880 | tf_op jit(solution)/shard_map/reduce_scatter | solution.py:125
  113.0 31.0 %copy-start.16 = (bf16[512,2048]{1,0:T(8,128)(2,1)S(1)}, bf16[512,2048]{1,0:T(8,128)(2,1)}, u32[]{:S(2)}) copy-start(bf16[512,2048]{1,0:T(8,128)(2,1)} %constant_dynamic-update-slice_fusion.12) | copy-start | bytes 6291460
  153.3 6.9 copy-start.11
  154.7 4.2 copy-start.24
  155.1 3.8 copy-start.22
  163.9 26.5 %copy-start.26 = (bf16[8,64,512]{2,1,0:T(8,128)(2,1)}, bf16[8,64,512]{2,1,0:T(8,128)(2,1)S(1)}, u32[]{:S(2)}) copy-start(bf16[8,64,512]{2,1,0:T(8,128)(2,1)S(1)} %fusion.29) | copy-start | bytes 1572868
  190.5 223.2 %all-gather.9.cloned.1.call-start = ((), (), s32[]{:S(2)}) async-start(), calls=%async_computation.17 | async-start | bytes 12976128 | tf_op jit(solution)/shard_map/all_gather | solution.py:104
  252.2 255.1 %all-gather.11.cloned.1.call-start = ((), (), s32[]{:S(2)}) async-start(), calls=%async_computation.18 | async-start | bytes 6488064 | tf_op jit(solution)/shard_map/all_gather | solution.py:105
  310.0 9.4 copy-start.50
  310.0 9.3 copy-start.49
  317.5 252.4 %reduce-scatter.11.cloned.1.call-start = ((), (), s32[]{:S(2)}) async-start(), calls=%async_computation.20 | async-start | bytes 5242880 | tf_op jit(solution)/shard_map/reduce_scatter | solution.py:125
  317.5 13.9 collective-permute-start.6
  317.6 23.1 %collective-permute-start.7 = (bf16[128,2048]{1,0:T(8,128)(2,1)S(1)}, bf16[128,2048]{1,0:T(8,128)(2,1)}, u32[]{:S(2)}, u32[]{:S(2)}) collective-permute-start(bf16[128,2048]{1,0:T(8,128)(2,1)S(1)} %copy-done.9), channel_id=1, source_target_pairs={{0,3},{1,0},{2,1},{3,2},{4,7},{5,4},{6,5},{7,6},{8,11},{9,8},{10,9... | collective-permute-start | bytes 1572872 | tf_op jit(solution)/shard_map/ppermute | solution.py:27
  331.4 17.3 collective-permute-start.8
  335.8 12.8 collective-permute-start.3
  339.0 11.4 collective-permute-start.4
  348.5 8.8 collective-permute-start.5
  507.4 12.0 copy-start.3
  527.0 89.9 %reduce-scatter.9.cloned.1.call-start = ((), (), s32[]{:S(2)}) async-start(), calls=%async_computation.19 | async-start | bytes 5242880 | tf_op jit(solution)/shard_map/reduce_scatter | solution.py:125
  535.7 211.3 %reduce-scatter.15.cloned.1.call-start = ((), (), s32[]{:S(2)}) async-start(), calls=%async_computation.22 | async-start | bytes 4718592 | tf_op jit(solution)/shard_map/reduce_scatter | solution.py:112
  619.6 13.8 copy-start.4
  619.9 23.5 %copy-start.27 = (bf16[8,64,512]{2,1,0:T(8,128)(2,1)S(1)}, bf16[8,64,512]{2,1,0:T(8,128)(2,1)}, u32[]{:S(2)}) copy-start(bf16[8,64,512]{2,1,0:T(8,128)(2,1)} %copy-done.26) | copy-start | bytes 1572868
  620.1 13.2 collective-permute-start.9
  620.2 13.2 collective-permute-start.10
  633.3 8.6 collective-permute-start.11
  646.7 283.9 %reduce-scatter.17.cloned.1.call-start = ((), (), s32[]{:S(2)}) async-start(), calls=%async_computation.23 | async-start | bytes 12976128 | tf_op jit(solution)/shard_map/reduce_scatter | solution.py:112
  655.9 1460.3 %all-reduce.18.cloned.1.call-start = ((), (), s32[]{:S(2)}) async-start(), calls=%async_computation.24 | async-start | bytes 79691776
  669.9 26.9 %copy-start.14 = (bf16[512,2048]{1,0:T(8,128)(2,1)S(1)}, bf16[512,2048]{1,0:T(8,128)(2,1)}, u32[]{:S(2)}) copy-start(bf16[512,2048]{1,0:T(8,128)(2,1)} %copy-done.13) | copy-start | bytes 6291460
  699.7 5.5 slice-start
  699.8 5.9 slice-start.1
  710.8 28.4 %copy-start.20 = (bf16[512,8,64]{0,2,1:T(8,128)(2,1)}, bf16[512,8,64]{0,2,1:T(8,128)(2,1)S(1)}, u32[]{:S(2)}) copy-start(bf16[512,8,64]{0,2,1:T(8,128)(2,1)S(1)} %get-tuple-element.68) | copy-start | bytes 1572868
  710.8 28.4 %copy-start.21 = (bf16[512,8,64]{0,2,1:T(8,128)(2,1)}, bf16[512,8,64]{0,2,1:T(8,128)(2,1)S(1)}, u32[]{:S(2)}) copy-start(bf16[512,8,64]{0,2,1:T(8,128)(2,1)S(1)} %get-tuple-element.69) | copy-start | bytes 1572868
  712.2 27.0 %copy-start.10 = (bf16[8,64,512]{2,1,0:T(8,128)(2,1)}, bf16[8,64,512]{2,1,0:T(8,128)(2,1)S(1)}, u32[]{:S(2)}) copy-start(bf16[8,64,512]{2,1,0:T(8,128)(2,1)S(1)} %fusion.30) | copy-start | bytes 1572868
  739.1 1437.1 %reduce-scatter.13.cloned.1.call-start = ((), (), s32[]{:S(2)}) async-start(), calls=%async_computation.21 | async-start | bytes 5242880 | tf_op jit(solution)/shard_map/reduce_scatter | solution.py:125
  749.4 185.1 %all-to-all-start.5 = ((f32[256,1,512]{2,1,0:T(1,128)}), f32[256,1,512]{2,1,0:T(1,128)S(1)}, u32[]{:S(2)}, u32[]{:S(2)}) async-start(f32[256,1,512]{2,1,0:T(1,128)} %copy.158), calls=%async_computation.10 | async-start | bytes 1048576 | tf_op jit(solution)/shard_map/all_to_all | solution.py:116
  752.9 186.0 %copy-start.59 = (u32[32]{0:T(128)S(1)}, u32[32]{0:T(128)}, u32[]{:S(2)}) copy-start(u32[32]{0:T(128)} %constant.120) | copy-start | bytes 388
  935.3 1184.2 %all-to-all-start.7 = ((f32[256,1,1408]{2,1,0:T(1,128)}), f32[256,1,1408]{2,1,0:T(1,128)S(1)}, u32[]{:S(2)}, u32[]{:S(2)}) async-start(f32[256,1,1408]{2,1,0:T(1,128)} %copy.161), calls=%async_computation.13 | async-start | bytes 2883584 | tf_op jit(solution)/shard_map/all_to_all | solution.py:116
  2120.6 41.2 %all-to-all-start.4 = ((f32[256,3,512]{2,1,0:T(4,128)}), f32[256,3,512]{2,1,0:T(4,128)S(1)}, u32[]{:S(2)}, u32[]{:S(2)}) async-start(f32[256,3,512]{2,1,0:T(4,128)} %constant_dynamic-slice_fusion.2), calls=%async_computation.8 | async-start | bytes 4194304 | tf_op jit(solution)/shard_map/all_to_all | solution.py:115
  2129.3 46.9 %copy-start.2 = (bf16[128,2048]{1,0:T(8,128)(2,1)S(1)}, bf16[128,2048]{1,0:T(8,128)(2,1)}, u32[]{:S(2)}) copy-start(bf16[128,2048]{1,0:T(8,128)(2,1)} %param.14) | copy-start | bytes 1572868
  2129.3 46.9 %copy-start.40 = (f32[2048]{0:T(1024)S(1)}, f32[2048]{0:T(1024)}, u32[]{:S(2)}) copy-start(f32[2048]{0:T(1024)} %copy-done.39) | copy-start | bytes 24580
  2129.3 46.9 %copy-start.45 = (f32[128]{0:T(128)S(1)}, f32[128]{0:T(128)}, u32[]{:S(2)}) copy-start(f32[128]{0:T(128)} %copy-done.44) | copy-start | bytes 1540
  2163.1 88.5 %all-to-all-start.6 = ((f32[256,2,1408]{2,1,0:T(2,128)}), f32[256,2,1408]{2,1,0:T(2,128)S(1)}, u32[]{:S(2)}, u32[]{:S(2)}) async-start(f32[256,2,1408]{2,1,0:T(2,128)} %constant_dynamic-slice_fusion.1), calls=%async_computation.11 | async-start | bytes 5767168 | tf_op jit(solution)/shard_map/all_to_all | solution.py:115
  2166.8 11.0 copy-start.53
  2166.8 11.0 copy-start.48
  2235.9 6.3 copy-start.19
  2238.9 4.6 copy-start.8
  (30 other events, 57.9 us)
Sparse Core Ops, SparseCore 0:
  34.3 100.8 all-gather.4
  137.9 47.6 all-gather.6
  190.6 58.4 reduce-scatter.6
  252.4 161.2 all-gather.8
  416.5 90.8 all-gather.10
  527.2 42.6 reduce-scatter.10
  572.4 44.4 reduce-scatter.8
  646.8 87.6 reduce-scatter.14
  738.1 192.4 reduce-scatter.16
  934.9 1181.2 all-reduce.17
  2118.7 57.4 reduce-scatter.12
